TPU v7x, 512 devices: a whole 4x8x8 slice. The times are simulated.
512 devices in a mesh: date: 32 (over z_hi, y, core), strip: 16 (over x, z_lo).
Axes of the slice: x: 4, y: 8, z: 8 (z_hi: 2, z_lo: 4; z = z_hi * 4 + z_lo), core: 2. Of those that a mesh axis runs over, the one named last changes fastest.
Arguments:
- slc: bfloat16 [2, 64, 512, 1024], P(None, 'date', 'strip')
- block_order: int32 [32], replicated, may hold values from 0 to 31, each once
- az_offset: int32 [128], P('strip'), may hold values from 0 to 3
- rg_offset: int32 [256], replicated, may hold values from 0 to 3
Outputs:
- coherence: float32 [2, 64, 64, 128, 256], P(None, 'date', None, 'strip')
Inputs may be any that keep to these rules, and one draw needn't show every extreme that they name: block_order is a permutation of the 32 chronological block numbers.
All inputs are finite; a program needn't handle non-finite values.
Results may differ from a plain program's by a relative error of at most 0.0003.
Values may be sent and summed in bfloat16 or wider, within the bound.
A program may use at most 64 MiB of HBM per device.

v0:
```python
import functools

import jax
import jax.numpy as jnp
from jax import lax
from jax.experimental import pallas as pl
from jax.experimental.pallas import tpu as pltpu
from jax.sharding import PartitionSpec as P

RG_WIN = 5
STEP = 4
HALO = 5
EPSILON = 1e-06
MESH = pl.DeviceIdType.MESH

CHUNKS = 8
COLUMN = 8

BLOCKS = [
    (0, 0, 0, 0), (0, 0, 0, 1),
    (0, 0, 1, 0), (0, 1, 1, 0), (0, 0, 1, 1), (0, 1, 1, 1),
    (0, 0, 2, 0), (0, 1, 2, 0), (0, 0, 2, 1), (0, 1, 2, 1),
    (1, 0, 0, 0), (1, 0, 0, 1),
    (0, 0, 3, 0), (0, 1, 3, 0), (0, 0, 3, 1), (0, 1, 3, 1),
    (1, 0, 1, 0), (1, 1, 1, 0), (1, 0, 1, 1), (1, 1, 1, 1),
    (0, 0, 4, 0), (0, 0, 4, 1),
    (1, 0, 2, 0), (1, 1, 2, 0), (1, 0, 2, 1), (1, 1, 2, 1),
    (1, 0, 3, 0), (1, 1, 3, 0), (1, 0, 3, 1), (1, 1, 3, 1),
    (1, 0, 4, 0), (1, 0, 4, 1),
]
SLOT = {block: place for place, block in enumerate(BLOCKS)}
EVENTS = {
    1: [("ring", 0, 1, 0)],
    2: [("ring", 0, 1, 1)],
    4: [("across", 0)],
    6: [("ring", 0, 2, 0), ("ring", 0, 2, 1)],
    8: [("across", 1)],
    10: [("ring", 1, 1, 0)],
    12: [("ring", 0, 3, 0), ("ring", 0, 3, 1)],
    14: [("ring", 1, 1, 1)],
    16: [("ring", 1, 2, 0)],
    20: [("ring", 0, 4, 0)],
    22: [("ring", 1, 2, 1)],
    24: [("ring", 1, 3, 0)],
    26: [("ring", 1, 3, 1)],
    30: [("ring", 1, 4, 0)],
}


def slot_of(row, direction, distance, sibling=0):
    return SLOT[(row, direction if 0 < distance < 4 else 0, distance, sibling)]


def body(
    order, az_offset, rg_offset, x, out,
    held, own, fields, sums, box, scale,
    ring_send, ring_recv, halo_send, halo_recv, across_send, across_recv,
    sib_send, sib_recv, edge_send, edge_recv, local_sem,
):
    date, strip = lax.axis_index("date"), lax.axis_index("strip")
    strips = lax.axis_size("strip")
    core, y, half = date % 2, (date // 2) % COLUMN, date // (2 * COLUMN)
    lines = x.shape[2]
    total = held.shape[3]

    def at(half_, y_, core_):
        return half_ * (2 * COLUMN) + ((y_ + COLUMN) % COLUMN) * 2 + core_

    upper, lower = (at(half, y + 1, core), strip), (at(half, y - 1, core), strip)
    facing, sibling = (at(1 - half, y, core), strip), (at(half, y, 1 - core), strip)
    after = (date, (strip + 1) % strips)
    before = (date, (strip + strips - 1) % strips)

    barrier = pltpu.get_barrier_semaphore()
    for target in (upper, lower, facing, sibling, after, before):
        pl.semaphore_signal(barrier, inc=1, device_id=target, device_id_type=MESH)
    pl.semaphore_wait(barrier, 6)

    def copy(src, dst, send, recv, target):
        return pltpu.make_async_remote_copy(
            src_ref=src, dst_ref=dst, send_sem=send, recv_sem=recv, device_id=target, device_id_type=MESH
        )

    def to_after():
        return copy(
            x.at[:, :, pl.ds(lines - HALO, HALO)], held.at[0, :, :, pl.ds(lines, HALO)],
            edge_send.at[0], edge_recv.at[0], after,
        )

    def to_before():
        return copy(
            x.at[:, :, pl.ds(0, HALO)], held.at[0, :, :, pl.ds(lines + HALO, HALO)],
            edge_send.at[1], edge_recv.at[1], before,
        )

    def ring(row, direction, distance, part):
        target = upper if direction == 0 else lower
        place = slot_of(row, direction, distance)
        index = (row, direction, distance - 1, part)
        send, recv = ring_send.at[index], ring_recv.at[index]
        if row == 0 and distance == 1 and part == 0:
            main = pl.ds(0, lines)
            return copy(x.at[0], held.at[place, 0, :, main], send, recv, target)
        source = slot_of(row, direction, distance - 1)
        return copy(held.at[source, part], held.at[place, part], send, recv, target)

    def ring_halo(direction):
        target = upper if direction == 0 else lower
        edge = pl.ds(lines, 2 * HALO)
        return copy(
            held.at[0, 0, :, edge], held.at[slot_of(0, direction, 1), 0, :, edge],
            halo_send.at[direction], halo_recv.at[direction], target,
        )

    def across(part):
        place = slot_of(1, 0, 0)
        send, recv = across_send.at[part], across_recv.at[part]
        if part == 0:
            return copy(x.at[0], held.at[place, 0, :, pl.ds(0, lines)], send, recv, facing)
        return copy(held.at[0, 1], held.at[place, 1], send, recv, facing)

    def across_halo():
        edge = pl.ds(lines, 2 * HALO)
        return copy(
            held.at[0, 0, :, edge], held.at[slot_of(1, 0, 0), 0, :, edge],
            halo_send.at[2], halo_recv.at[2], facing,
        )

    def beside(row, direction, distance, part):
        source, place = slot_of(row, direction, distance), slot_of(row, direction, distance, 1)
        send, recv = sib_send.at[place, part], sib_recv.at[place, part]
        if source == 0 and part == 0:
            return copy(x.at[0], held.at[place, 0, :, pl.ds(0, lines)], send, recv, sibling)
        return copy(held.at[source, part], held.at[place, part], send, recv, sibling)

    def beside_halo():
        edge = pl.ds(lines, 2 * HALO)
        return copy(
            held.at[0, 0, :, edge], held.at[1, 0, :, edge], halo_send.at[3], halo_recv.at[3], sibling
        )

    def parts_of(direction, distance):
        return (0, 1) if distance < 4 else (direction,)

    def start_ring(row, distance, part):
        for direction in (0, 1):
            if part in parts_of(direction, distance):
                ring(row, direction, distance, part).start()

    def event(kind, *what):
        if kind == "across":
            (part,) = what
            across(part).wait_recv()
            if part == 0:
                across_halo().wait_recv()
            start_ring(1, 1, part)
            beside(1, 0, 0, part).start()
            return
        row, distance, part = what
        for direction in (0, 1):
            if distance == 4:
                part = direction
            ring(row, direction, distance, part).wait_recv()
            if row == 0 and distance == 1 and part == 0:
                ring_halo(direction).wait_recv()
            if distance < 4 and part in parts_of(direction, distance + 1):
                ring(row, direction, distance + 1, part).start()
            beside(row, direction, distance, part).start()

    to_after().start()
    to_before().start()
    local = pltpu.make_async_copy(x, held.at[0, :, :, pl.ds(0, lines)], local_sem)
    local.start()
    across(0).start()
    start_ring(0, 1, 0)
    beside(0, 0, 0, 0).start()

    columns = box.shape[1]
    sample = lax.broadcasted_iota(jnp.int32, (128, columns), 0)
    centre = STEP * lax.broadcasted_iota(jnp.int32, (128, columns), 1) + rg_offset[...]
    for chunk in range(CHUNKS):
        inside = jnp.abs(sample + 128 * chunk - centre) <= RG_WIN // 2
        box[pl.ds(128 * chunk, 128), :] = jnp.where(inside, 1.0, 0.0).astype(jnp.bfloat16)

    local.wait()
    to_after().wait_recv()
    to_before().wait_recv()

    @pl.when(strip == 0)
    def _():
        held[0, :, :, lines : lines + HALO] = jnp.zeros((2, 2, HALO, CHUNKS, 128), held.dtype)

    @pl.when(strip == strips - 1)
    def _():
        held[0, :, :, lines + HALO :] = jnp.zeros((2, 2, HALO, CHUNKS, 128), held.dtype)

    across_halo().start()
    for direction in (0, 1):
        ring_halo(direction).start()
    beside_halo().start()
    across(1).start()
    start_ring(0, 1, 1)
    beside(0, 0, 0, 1).start()

    for part in (0, 1):
        for mine in (0, 1):
            own[part, mine] = held[0, part, mine].astype(jnp.float32)

    spans = [(first, 4, first + HALO) for first in range(0, lines, 4)]
    spans += [(lines, HALO, 0), (lines + HALO, HALO, lines + HALO)]

    def work(step, carry):
        for place, events in EVENTS.items():

            @pl.when(step == place)
            def _():
                for one in events:
                    event(*one)

        for place, (row, direction, distance, side) in enumerate(BLOCKS):
            if side:

                @pl.when(step == place)
                def _():
                    parts = (0, 1)
                    for part in parts:
                        beside(row, direction, distance, part).wait_recv()
                    if place == 1:
                        beside_halo().wait_recv()

        block = 0
        for place, (row, direction, distance, side) in enumerate(BLOCKS):
            y_ = y - distance if direction == 0 else y + distance
            index = at(1 - half if row else half, y_, 1 - core if side else core)
            block = jnp.where(step == place, index, block)

        def one_date(other, inner):
            for first, count, place in spans:
                here = pl.ds(first, count)
                there = pl.ds(place, count)
                b_re = held[step, 0, other, here].astype(jnp.float32)
                b_im = held[step, 1, other, here].astype(jnp.float32)
                for mine in (0, 1):
                    a_re, a_im = own[0, mine, here], own[1, mine, here]
                    fields[2 * mine, there] = a_re * b_re + a_im * b_im
                    fields[2 * mine + 1, there] = a_im * b_re - a_re * b_im
                fields[4, there] = b_re * b_re + b_im * b_im
            for o in range(lines // STEP):
                start = az_offset[o] + STEP * o
                for f in range(5):
                    window = jnp.sum(fields[f, pl.ds(start, 2 * HALO + 1)], axis=0)
                    sums[pl.ds(pl.multiple_of(other * 320 + f * 64 + o * 8, 8), 8), :] = window
            return inner

        lax.fori_loop(0, 2, one_date, 0)
        wide = jnp.concatenate([sums[pl.ds(chunk, 80, stride=CHUNKS), :] for chunk in range(CHUNKS)], axis=1)
        high = wide.astype(jnp.bfloat16)
        low = (wide - high.astype(jnp.float32)).astype(jnp.bfloat16)
        both = jnp.dot(jnp.concatenate([high, low], axis=0), box[...], preferred_element_type=jnp.float32)
        cross = both[:80] + both[80:]
        others = [lax.rsqrt(cross[40 * other + 32 : 40 * other + 40] + EPSILON) for other in (0, 1)]

        @pl.when(step == 0)
        def _():
            for mine in (0, 1):
                scale[mine] = others[mine]

        for mine in (0, 1):
            mine_scale = scale[mine]
            for other in (0, 1):
                later = order[block] * 2 + other > order[date] * 2 + mine
                for part in (0, 1):
                    first = 40 * other + 16 * mine + 8 * part
                    value = cross[first : first + 8] * mine_scale * others[other]
                    out[part, mine, block * 2 + other] = jnp.where(later, value, 0.0)
        return carry

    lax.fori_loop(0, len(BLOCKS), work, 0)

    to_after().wait_send()
    to_before().wait_send()
    for direction in (0, 1):
        ring_halo(direction).wait_send()
        for row in (0, 1):
            for distance in (1, 2, 3, 4):
                for part in parts_of(direction, distance):
                    ring(row, direction, distance, part).wait_send()
                    beside(row, direction, distance, part).wait_send()
    across_halo().wait_send()
    beside_halo().wait_send()
    for part in (0, 1):
        across(part).wait_send()
        for row in (0, 1):
            beside(row, 0, 0, part).wait_send()


def on_device(slc, block_order, az_offset, rg_offset):
    parts, dates, lines, samples = slc.shape
    rows, columns = lines // STEP, samples // STEP
    count = block_order.shape[0]
    total = lines + 2 * HALO
    vmem = pl.BlockSpec(memory_space=pltpu.VMEM)
    smem = pl.BlockSpec(memory_space=pltpu.SMEM)
    dma = pltpu.SemaphoreType.DMA
    return pl.pallas_call(
        body,
        out_shape=jax.ShapeDtypeStruct((2, dates, dates * count, rows, columns), jnp.float32),
        in_specs=[smem, smem, vmem, vmem],
        out_specs=vmem,
        scratch_shapes=[
            pltpu.VMEM((count, 2, dates, total, CHUNKS, 128), jnp.bfloat16),
            pltpu.VMEM((2, dates, total, CHUNKS, 128), jnp.float32),
            pltpu.VMEM((5, total, CHUNKS, 128), jnp.float32),
            pltpu.VMEM((2 * 5 * rows * CHUNKS, 128), jnp.float32),
            pltpu.VMEM((samples, columns), jnp.bfloat16),
            pltpu.VMEM((dates, rows, columns), jnp.float32),
            dma((2, 2, 4, 2)), dma((2, 2, 4, 2)),
            dma((4,)), dma((4,)),
            dma((2,)), dma((2,)),
            dma((count, 2)), dma((count, 2)),
            dma((2,)), dma((2,)),
            dma,
        ],
        compiler_params=pltpu.CompilerParams(
            collective_id=0, has_side_effects=True, vmem_limit_bytes=48 * 2**20
        ),
    )(block_order, az_offset, rg_offset[None], slc.reshape(parts, dates, lines, CHUNKS, 128))


def solution(mesh):
    placed = (P(None, "date", "strip", None), P(), P("strip"), P())
    return jax.shard_map(
        on_device,
        mesh=mesh,
        in_specs=placed,
        out_specs=P(None, "date", None, "strip", None),
        check_vma=False,
    )
```

profile of v0, /device:TPU:1, one launch (start us, length us, event | category | flops | bytes accessed | tf_op | source)
XLA Modules:
  0.0 81.9 jit_solution(10461093651904108597)
XLA Ops:
  0.0 1.0 %copy.5 = bf16[16,8,8,128]{3,2,1,0:T(8,128)(2,1)S(1)} copy(bf16[16,8,8,128]{3,1,2,0:T(8,128)(2,1)} %bitcast.8) | data formatting | bytes 524288
  1.0 0.0 copy-start
  1.0 0.7 copy-done
  1.7 0.0 copy-start.1
  1.7 0.7 copy-done.1
  2.3 0.0 copy-start.2
  2.3 0.7 copy-done.2
  3.0 77.6 %shard_map.46 = f32[2,2,64,8,256]{4,3,2,1,0:T(8,128)S(1)} custom-call(s32[32]{0:T(128)S(1)} %copy-done.1, s32[8]{0:T(128)S(1)} %copy-done.2, s32[1,256]{1,0:T(1,128)S(1)} %bitcast.7, bf16[2,2,32,8,128]{4,3,2,1,0:T(8,128)(2,1)S(1)} %bitcast.6), custom_call_target="tpu_custom_call" | custom-call | tf_op jit(solution)/shard_map/pallas_call | solution.py:305
  80.6 1.3 %copy.7 = f32[2,2,64,8,256]{4,3,2,1,0:T(8,128)} copy(f32[2,2,64,8,256]{4,3,2,1,0:T(8,128)S(1)} %shard_map.46) | data formatting | bytes 4194304
Async XLA Ops:
  1.0 0.7 copy-start
  1.7 0.7 copy-start.1
  2.3 0.7 copy-start.2
where the time goes:
time: 82.1 us; the launch traced here: 81.9 us
  Pallas kernels  77.6 us (95%)
  local copies, waits for them, and re-layouts  4.3 us (5%)
    pallas_call x1, Pallas kernels, on_device(): pl.pallas_call(body, out_shape=jax.ShapeDtypeStruct((2, dates, dates * co...  77.6 us
    unnamed x8, local copies, waits for them, and re-layouts  4.3 us

commit v1 on v0

v1 whole, which is shorter than its diff:
```python
import functools

import jax
import jax.numpy as jnp
from jax import lax
from jax.experimental import pallas as pl
from jax.experimental.pallas import tpu as pltpu
from jax.sharding import PartitionSpec as P

RG_WIN = 5
STEP = 4
HALO = 5
EPSILON = 1e-06
MESH = pl.DeviceIdType.MESH

CHUNKS = 8
COLUMN = 8

BLOCKS = [
    (0, 0, 0, 0), (0, 0, 0, 1),
    (0, 0, 1, 0), (0, 1, 1, 0), (0, 0, 1, 1), (0, 1, 1, 1),
    (0, 0, 2, 0), (0, 1, 2, 0), (0, 0, 2, 1), (0, 1, 2, 1),
    (1, 0, 0, 0), (1, 0, 0, 1),
    (0, 0, 3, 0), (0, 1, 3, 0), (0, 0, 3, 1), (0, 1, 3, 1),
    (1, 0, 1, 0), (1, 1, 1, 0), (1, 0, 1, 1), (1, 1, 1, 1),
    (0, 0, 4, 0), (0, 0, 4, 1),
    (1, 0, 2, 0), (1, 1, 2, 0), (1, 0, 2, 1), (1, 1, 2, 1),
    (1, 0, 3, 0), (1, 1, 3, 0), (1, 0, 3, 1), (1, 1, 3, 1),
    (1, 0, 4, 0), (1, 0, 4, 1),
]
SLOT = {block: place for place, block in enumerate(BLOCKS)}
FIRST = -2
LAG = 10
EVENTS = {
    -2: [("ring", 0, 1, 0)],
    -1: [("ring", 0, 1, 1)],
    0: [("offsets",)],
    2: [("across", 0)],
    3: [("ring", 0, 2, 0)],
    4: [("ring", 0, 2, 1)],
    6: [("across", 1)],
    8: [("ring", 1, 1, 0)],
    10: [("ring", 0, 3, 0)],
    12: [("ring", 0, 3, 1)],
    14: [("ring", 1, 1, 1)],
    16: [("ring", 1, 2, 0)],
    19: [("ring", 0, 4, 0)],
    21: [("ring", 1, 2, 1)],
    24: [("ring", 1, 3, 0)],
    26: [("ring", 1, 3, 1)],
    30: [("ring", 1, 4, 0)],
}
for place, (row, direction, distance, sibling) in enumerate(BLOCKS):
    if sibling:
        EVENTS.setdefault(place, []).append(("beside", row, direction, distance))


def slot_of(row, direction, distance, sibling=0):
    return SLOT[(row, direction if 0 < distance < 4 else 0, distance, sibling)]


def picked(place, values):
    while len(values) > 1:
        odd = place % 2 == 1
        values = [jnp.where(odd, high, low) for low, high in zip(values[::2], values[1::2])]
        place = place // 2
    return values[0]


def body(
    small, x, out,
    held, own, fields, sums, box, scale, cross, from_before, from_after,
    numbers, my_offsets, next_offsets, last_offsets,
    ring_send, ring_recv, across_send, across_recv, sib_send, sib_recv, offset_send, offset_recv,
    part_send, part_recv, local_sem,
):
    date, strip = lax.axis_index("date"), lax.axis_index("strip")
    strips = lax.axis_size("strip")
    core, y, half = date % 2, (date // 2) % COLUMN, date // (2 * COLUMN)
    lines = x.shape[2]
    rows, columns = lines // STEP, box.shape[1]
    first_az = columns + len(BLOCKS)

    def at(half_, y_, core_):
        return half_ * (2 * COLUMN) + ((y_ + COLUMN) % COLUMN) * 2 + core_

    upper, lower = (at(half, y + 1, core), strip), (at(half, y - 1, core), strip)
    facing, sibling = (at(1 - half, y, core), strip), (at(half, y, 1 - core), strip)
    after = (date, (strip + 1) % strips)
    before = (date, (strip + strips - 1) % strips)

    to_scalars = pltpu.make_async_copy(small, numbers, local_sem.at[1])
    to_scalars.start()
    barrier = pltpu.get_barrier_semaphore()
    for target in (upper, lower, facing, sibling, after, before):
        pl.semaphore_signal(barrier, inc=1, device_id=target, device_id_type=MESH)
    pl.semaphore_wait(barrier, 6)

    def copy(src, dst, send, recv, target):
        return pltpu.make_async_remote_copy(
            src_ref=src, dst_ref=dst, send_sem=send, recv_sem=recv, device_id=target, device_id_type=MESH
        )

    def offset(which):
        send, recv = offset_send.at[which], offset_recv.at[which]
        if which == 0:
            return copy(my_offsets.at[pl.ds(2, 2)], last_offsets, send, recv, after)
        return copy(my_offsets.at[pl.ds(0, 2)], next_offsets, send, recv, before)

    def source_of(row, direction, distance, part):
        if row == 0 and distance == 0:
            return x.at[part]
        return held.at[slot_of(row, direction, distance), part]

    def ring(row, direction, distance, part):
        target = upper if direction == 0 else lower
        index = (row, direction, distance - 1, part)
        return copy(
            source_of(row, direction, distance - 1, part), held.at[slot_of(row, direction, distance), part],
            ring_send.at[index], ring_recv.at[index], target,
        )

    def across(part):
        return copy(
            x.at[part], held.at[slot_of(1, 0, 0), part], across_send.at[part], across_recv.at[part], facing
        )

    def beside(row, direction, distance, part):
        place = slot_of(row, direction, distance, 1)
        return copy(
            source_of(row, direction, distance, part), held.at[place, part],
            sib_send.at[place, part], sib_recv.at[place, part], sibling,
        )

    def to_after(place):
        return copy(
            cross.at[place, pl.ds(80, 24)], from_before.at[place], part_send.at[0, place], part_recv.at[0, place],
            after,
        )

    def to_before(place):
        return copy(
            cross.at[place, pl.ds(104, 24)], from_after.at[place], part_send.at[1, place], part_recv.at[1, place],
            before,
        )

    def parts_of(direction, distance):
        return (0, 1) if distance < 4 else (direction,)

    local = pltpu.make_async_copy(x, held.at[0], local_sem.at[0])

    def event(kind, *what):
        if kind == "offsets":
            offset(0).wait_recv()
            offset(1).wait_recv()
            local.wait()
        elif kind == "across":
            (part,) = what
            across(part).wait_recv()
            for direction in (0, 1):
                ring(1, direction, 1, part).start()
            beside(1, 0, 0, part).start()
        elif kind == "ring":
            row, distance, part = what
            for direction in (0, 1):
                if distance == 4:
                    part = direction
                ring(row, direction, distance, part).wait_recv()
                if distance < 4 and part in parts_of(direction, distance + 1):
                    ring(row, direction, distance + 1, part).start()
                beside(row, direction, distance, part).start()
        else:
            for part in (0, 1):
                beside(*what, part).wait_recv()

    for part in (0, 1):
        across(part).start()
        for direction in (0, 1):
            ring(0, direction, 1, part).start()
    local.start()
    for part in (0, 1):
        beside(0, 0, 0, part).start()
    to_scalars.wait()

    def az_offset(o):
        return numbers[0, first_az + o]

    for which, o in enumerate((0, 1, rows - 2, rows - 1)):
        my_offsets[which] = jnp.full((8, 128), az_offset(o), jnp.int32).astype(jnp.float32)
    offset(0).start()
    offset(1).start()

    sample = lax.broadcasted_iota(jnp.int32, (128, columns), 0)
    centre = STEP * lax.broadcasted_iota(jnp.int32, (128, columns), 1) + small[:, :columns]
    for chunk in range(CHUNKS):
        inside = jnp.abs(sample + 128 * chunk - centre) <= RG_WIN // 2
        box[pl.ds(128 * chunk, 128), :] = jnp.where(inside, 1.0, 0.0).astype(jnp.bfloat16)
    nothing = jnp.zeros((HALO, CHUNKS, 128), jnp.float32)
    for f in range(5):
        fields[f, 0:HALO] = nothing
        fields[f, lines + HALO :] = nothing
    sums[80 * 8 :, :] = jnp.zeros((48 * 8, 128), jnp.float32)
    for part in (0, 1):
        for mine in (0, 1):
            own[part, mine] = x[part, mine].astype(jnp.float32)

    def steps(step, low, high):
        here = [place for place in EVENTS if low <= place < high]
        if high - low == 1 or not here:
            for place in here:
                for one in EVENTS[place]:
                    event(*one)
            return
        middle = (low + high) // 2

        @pl.when(step < middle)
        def _():
            steps(step, low, middle)

        @pl.when(step >= middle)
        def _():
            steps(step, middle, high)

    def one_step(step, carry):
        @pl.when(step < len(BLOCKS))
        def _():
            steps(step, FIRST, len(BLOCKS))

        @pl.when(jnp.logical_and(step >= 0, step < len(BLOCKS)))
        def _():
            own_sums(step)

        @pl.when(step >= LAG)
        def _():
            finish(step - LAG)

        return carry

    def own_sums(place):
        def one_date(other, inner):
            for first in range(0, lines, 4):
                here, there = pl.ds(first, 4), pl.ds(first + HALO, 4)
                b_re = held[place, 0, other, here].astype(jnp.float32)
                b_im = held[place, 1, other, here].astype(jnp.float32)
                for mine in (0, 1):
                    a_re, a_im = own[0, mine, here], own[1, mine, here]
                    fields[2 * mine, there] = a_re * b_re + a_im * b_im
                    fields[2 * mine + 1, there] = a_im * b_re - a_re * b_im
                fields[4, there] = b_re * b_re + b_im * b_im
            for o in range(rows):
                start = az_offset(o) + STEP * o
                for f in range(5):
                    window = jnp.sum(fields[f, pl.ds(start, 2 * HALO + 1)], axis=0)
                    sums[pl.ds(pl.multiple_of(other * 320 + f * 64 + o * 8, 8), 8), :] = window
            ahead, ahead_second = next_offsets[0], next_offsets[1]
            sixth, seventh = last_offsets[0], last_offsets[1]
            for f in range(5):
                line = [fields[f, HALO + l] for l in range(HALO)]
                near = line[0] + line[1]
                for l in (2, 3, 4):
                    near = near + jnp.where(seventh >= l - 1, line[l], 0.0)
                single = jnp.where(sixth >= 3, line[0], 0.0)
                line = [fields[f, lines + l] for l in range(HALO)]
                far = line[3] + line[4]
                for l in (0, 1, 2):
                    far = far + jnp.where(ahead <= l, line[l], 0.0)
                far_second = jnp.where(ahead_second <= 0, line[4], 0.0)
                for group, value in ((80, far), (90, far_second), (104, single), (114, near)):
                    sums[pl.ds(pl.multiple_of((group + other * 5 + f) * 8, 8), 8), :] = value
            return inner

        lax.fori_loop(0, 2, one_date, 0)
        wide = jnp.concatenate([sums[pl.ds(chunk, 128, stride=CHUNKS), :] for chunk in range(CHUNKS)], axis=1)
        high = wide.astype(jnp.bfloat16)
        low = (wide - high.astype(jnp.float32)).astype(jnp.bfloat16)
        both = jnp.dot(jnp.concatenate([high, low], axis=0), box[...], preferred_element_type=jnp.float32)
        cross[place] = both[:128] + both[128:]
        to_after(place).start()
        to_before(place).start()

    sub = lax.broadcasted_iota(jnp.int32, (rows, columns), 0)
    top = jnp.logical_and(sub == 0, strip > 0)
    second = jnp.logical_and(sub == 1, strip > 0)
    next_last = jnp.logical_and(sub == rows - 2, strip < strips - 1)
    last = jnp.logical_and(sub == rows - 1, strip < strips - 1)
    indices = []
    for row, direction, distance, side in BLOCKS:
        y_ = y - distance if direction == 0 else y + distance
        indices.append(at(1 - half if row else half, y_, 1 - core if side else core))

    def finish(place):
        block = picked(place, indices)
        to_after(place).wait_recv()
        to_before(place).wait_recv()

        def whole(f):
            value = cross[place, 8 * f : 8 * f + 8]
            value = value + jnp.where(top, from_before[place, f : f + 1], 0.0)
            value = value + jnp.where(second, from_before[place, 10 + f : 11 + f], 0.0)
            value = value + jnp.where(next_last, from_after[place, f : f + 1], 0.0)
            return value + jnp.where(last, from_after[place, 10 + f : 11 + f], 0.0)

        others = [lax.rsqrt(whole(5 * other + 4) + EPSILON) for other in (0, 1)]

        @pl.when(place == 0)
        def _():
            for mine in (0, 1):
                scale[mine] = others[mine]

        for mine in (0, 1):
            mine_scale = scale[mine]
            for other in (0, 1):
                later = numbers[0, columns + block] * 2 + other > numbers[0, columns + date] * 2 + mine
                for part in (0, 1):
                    value = whole(5 * other + 2 * mine + part) * mine_scale * others[other]
                    out[part, mine, block * 2 + other] = jnp.where(later, value, 0.0)

    lax.fori_loop(0, len(BLOCKS) + LAG - FIRST, lambda n, c: one_step(n + FIRST, c), 0)

    for which in (0, 1):
        offset(which).wait_send()
        across(which).wait_send()
    for row in (0, 1):
        for distance in range(5):
            for direction in (0, 1) if distance else (0,):
                for part in parts_of(direction, distance):
                    if distance:
                        ring(row, direction, distance, part).wait_send()
                    beside(row, direction, distance, part).wait_send()

    def sent(place, carry):
        to_after(place).wait_send()
        to_before(place).wait_send()
        return carry

    lax.fori_loop(0, len(BLOCKS), sent, 0)


def on_device(slc, block_order, az_offset, rg_offset):
    parts, dates, lines, samples = slc.shape
    rows, columns = lines // STEP, samples // STEP
    count = block_order.shape[0]
    total = lines + 2 * HALO
    vmem = pl.BlockSpec(memory_space=pltpu.VMEM)
    dma = pltpu.SemaphoreType.DMA
    tile = (CHUNKS, 128)
    small = jnp.concatenate([rg_offset, block_order, az_offset])
    width = -(-small.shape[0] // 128) * 128
    small = jnp.pad(small, (0, width - small.shape[0]))[None]
    return pl.pallas_call(
        body,
        out_shape=jax.ShapeDtypeStruct((2, dates, dates * count, rows, columns), jnp.float32),
        in_specs=[vmem, vmem],
        out_specs=vmem,
        scratch_shapes=[
            pltpu.VMEM((count, 2, dates, lines, *tile), jnp.bfloat16),
            pltpu.VMEM((2, dates, lines, *tile), jnp.float32),
            pltpu.VMEM((5, total, *tile), jnp.float32),
            pltpu.VMEM((128 * CHUNKS, 128), jnp.float32),
            pltpu.VMEM((samples, columns), jnp.bfloat16),
            pltpu.VMEM((dates, rows, columns), jnp.float32),
            pltpu.VMEM((count, 128, columns), jnp.float32),
            pltpu.VMEM((count, 24, columns), jnp.float32),
            pltpu.VMEM((count, 24, columns), jnp.float32),
            pltpu.SMEM((1, width), jnp.int32),
            pltpu.VMEM((4, 8, 128), jnp.float32),
            pltpu.VMEM((2, 8, 128), jnp.float32),
            pltpu.VMEM((2, 8, 128), jnp.float32),
            dma((2, 2, 4, 2)), dma((2, 2, 4, 2)),
            dma((2,)), dma((2,)),
            dma((count, 2)), dma((count, 2)),
            dma((2,)), dma((2,)),
            dma((2, count)), dma((2, count)),
            dma((2,)),
        ],
        compiler_params=pltpu.CompilerParams(
            collective_id=0, has_side_effects=True, vmem_limit_bytes=48 * 2**20
        ),
    )(small, slc.reshape(parts, dates, lines, *tile))


def solution(mesh):
    placed = (P(None, "date", "strip", None), P(), P("strip"), P())
    return jax.shard_map(
        on_device,
        mesh=mesh,
        in_specs=placed,
        out_specs=P(None, "date", None, "strip", None),
        check_vma=False,
    )
```

time: 82.1 us -> 74.3 us (0.905)
  Pallas kernels: 77.6 us -> 71.1 us
  local copies, waits for them, and re-layouts: 4.3 us -> 2.32 us
    pallas_call x1, Pallas kernels: 77.6 us -> 71.1 us  [on_device(): pl.pallas_call(body, out_shape=jax.ShapeDtypeStruct((2, dates, dates * co...]
    unnamed x8 -> x2, local copies, waits for them, and re-layouts: 4.3 us -> 2.31 us
where the time goes in v1:
time: 74.3 us; the launch traced here: 74.2 us
  Pallas kernels  71.1 us (96%)
  local copies, waits for them, and re-layouts  2.32 us (3%)
  other arithmetic  0.79 us (1%)
    pallas_call x1, Pallas kernels, on_device(): pl.pallas_call(body, out_shape=jax.ShapeDtypeStruct((2, dates, dates * co...  71.1 us
    unnamed x2, local copies, waits for them, and re-layouts  2.31 us

profile of v1, /device:TPU:1, one launch (start us, length us, event | category | flops | bytes accessed | tf_op | source)
XLA Modules:
  0.0 74.2 jit_solution(15776229965979945319)
XLA Ops:
  0.0 0.8 %pad_add_fusion = s32[296]{0:T(512)S(1)} fusion(s32[8]{0:T(128)} %param.6, s32[32]{0:T(128)} %param.5, s32[256]{0:T(256)} %param.7), kind=kLoop, calls=%fused_computation | loop fusion | flops 592 | bytes 2368 | tf_op jit(solution)/shard_map/concatenate | solution.py:347
  0.8 1.0 %copy.5 = bf16[16,8,8,128]{3,2,1,0:T(8,128)(2,1)S(1)} copy(bf16[16,8,8,128]{3,1,2,0:T(8,128)(2,1)} %bitcast.6) | data formatting | bytes 524288
  1.8 71.1 %shard_map.46 = f32[2,2,64,8,256]{4,3,2,1,0:T(8,128)S(1)} custom-call(s32[1,384]{1,0:T(1,128)S(1)} %broadcast_in_dim.3.small, bf16[2,2,32,8,128]{4,3,2,1,0:T(8,128)(2,1)S(1)} %bitcast.5), custom_call_target="tpu_custom_call" | custom-call | tf_op jit(solution)/shard_map/pallas_call | solution.py:350
  72.9 1.3 %copy.7 = f32[2,2,64,8,256]{4,3,2,1,0:T(8,128)} copy(f32[2,2,64,8,256]{4,3,2,1,0:T(8,128)S(1)} %shard_map.46) | data formatting | bytes 4194304
  (2 shorter events, 0.0 us)

commit v2 on v1

--- a/solution.py
+++ b/solution.py
@@ -69,8 +69,8 @@
 
 def body(
     small, x, out,
-    held, own, fields, sums, box, scale, cross, from_before, from_after,
-    numbers, my_offsets, next_offsets, last_offsets,
+    held, own, fields, quads, sums, box, scale, cross, from_before, from_after,
+    numbers, outer, my_offsets, next_offsets, last_offsets,
     ring_send, ring_recv, across_send, across_recv, sib_send, sib_recv, offset_send, offset_recv,
     part_send, part_recv, local_sem,
 ):
@@ -125,12 +125,10 @@
             x.at[part], held.at[slot_of(1, 0, 0), part], across_send.at[part], across_recv.at[part], facing
         )
 
-    def beside(row, direction, distance, part):
+    def beside(row, direction, distance):
         place = slot_of(row, direction, distance, 1)
-        return copy(
-            source_of(row, direction, distance, part), held.at[place, part],
-            sib_send.at[place, part], sib_recv.at[place, part], sibling,
-        )
+        source = x if row == 0 and distance == 0 else held.at[slot_of(row, direction, distance)]
+        return copy(source, held.at[place], sib_send.at[place], sib_recv.at[place], sibling)
 
     def to_after(place):
         return copy(
@@ -159,7 +157,8 @@
             across(part).wait_recv()
             for direction in (0, 1):
                 ring(1, direction, 1, part).start()
-            beside(1, 0, 0, part).start()
+            if part == 1:
+                beside(1, 0, 0).start()
         elif kind == "ring":
             row, distance, part = what
             for direction in (0, 1):
@@ -168,18 +167,17 @@
                 ring(row, direction, distance, part).wait_recv()
                 if distance < 4 and part in parts_of(direction, distance + 1):
                     ring(row, direction, distance + 1, part).start()
-                beside(row, direction, distance, part).start()
+                if part == 1 and (distance < 4 or direction == 1):
+                    beside(row, direction, distance).start()
         else:
-            for part in (0, 1):
-                beside(*what, part).wait_recv()
+            beside(*what).wait_recv()
 
     for part in (0, 1):
         across(part).start()
         for direction in (0, 1):
             ring(0, direction, 1, part).start()
     local.start()
-    for part in (0, 1):
-        beside(0, 0, 0, part).start()
+    beside(0, 0, 0).start()
     to_scalars.wait()
 
     def az_offset(o):
@@ -196,9 +194,14 @@
         inside = jnp.abs(sample + 128 * chunk - centre) <= RG_WIN // 2
         box[pl.ds(128 * chunk, 128), :] = jnp.where(inside, 1.0, 0.0).astype(jnp.bfloat16)
     nothing = jnp.zeros((HALO, CHUNKS, 128), jnp.float32)
-    for f in range(5):
-        fields[f, 0:HALO] = nothing
-        fields[f, lines + HALO :] = nothing
+    for other in (0, 1):
+        for f in range(5):
+            fields[other, f, 0:HALO] = nothing
+            fields[other, f, lines + HALO :] = nothing
+    spans = [(0, 2)] + [(first, 4) for first in range(2, lines - 2, 4)] + [(lines - 2, 2)]
+    for o in range(rows):
+        for k in range(3):
+            outer[3 * o + k] = STEP * o + k + jnp.where(az_offset(o) > k, 2 * HALO + 1, 0)
     sums[80 * 8 :, :] = jnp.zeros((48 * 8, 128), jnp.float32)
     for part in (0, 1):
         for mine in (0, 1):
@@ -237,39 +240,42 @@
         return carry
 
     def own_sums(place):
-        def one_date(other, inner):
-            for first in range(0, lines, 4):
-                here, there = pl.ds(first, 4), pl.ds(first + HALO, 4)
+        for quad, (first, count) in enumerate(spans):
+            here, there = pl.ds(first, count), pl.ds(first + HALO, count)
+            mines = [(own[0, mine, here], own[1, mine, here]) for mine in (0, 1)]
+            for other in (0, 1):
                 b_re = held[place, 0, other, here].astype(jnp.float32)
                 b_im = held[place, 1, other, here].astype(jnp.float32)
-                for mine in (0, 1):
-                    a_re, a_im = own[0, mine, here], own[1, mine, here]
-                    fields[2 * mine, there] = a_re * b_re + a_im * b_im
-                    fields[2 * mine + 1, there] = a_im * b_re - a_re * b_im
-                fields[4, there] = b_re * b_re + b_im * b_im
-            for o in range(rows):
-                start = az_offset(o) + STEP * o
-                for f in range(5):
-                    window = jnp.sum(fields[f, pl.ds(start, 2 * HALO + 1)], axis=0)
-                    sums[pl.ds(pl.multiple_of(other * 320 + f * 64 + o * 8, 8), 8), :] = window
-            ahead, ahead_second = next_offsets[0], next_offsets[1]
-            sixth, seventh = last_offsets[0], last_offsets[1]
+                values = []
+                for a_re, a_im in mines:
+                    values += [a_re * b_re + a_im * b_im, a_im * b_re - a_re * b_im]
+                values.append(b_re * b_re + b_im * b_im)
+                for f, value in enumerate(values):
+                    fields[other, f, there] = value
+                    quads[other, f, quad] = jnp.sum(value, axis=0)
+        ahead, ahead_second = next_offsets[0], next_offsets[1]
+        sixth, seventh = last_offsets[0], last_offsets[1]
+        for other in (0, 1):
             for f in range(5):
-                line = [fields[f, HALO + l] for l in range(HALO)]
+                quad = [quads[other, f, m] for m in range(rows + 1)]
+                for o in range(rows):
+                    window = quad[o] + quad[o + 1]
+                    for k in range(3):
+                        window = window + fields[other, f, outer[3 * o + k]]
+                    sums[pl.ds(other * 320 + f * 64 + o * 8, 8), :] = window
+                line = [fields[other, f, HALO + l] for l in range(HALO)]
                 near = line[0] + line[1]
                 for l in (2, 3, 4):
                     near = near + jnp.where(seventh >= l - 1, line[l], 0.0)
                 single = jnp.where(sixth >= 3, line[0], 0.0)
-                line = [fields[f, lines + l] for l in range(HALO)]
+                line = [fields[other, f, lines + l] for l in range(HALO)]
                 far = line[3] + line[4]
                 for l in (0, 1, 2):
                     far = far + jnp.where(ahead <= l, line[l], 0.0)
                 far_second = jnp.where(ahead_second <= 0, line[4], 0.0)
                 for group, value in ((80, far), (90, far_second), (104, single), (114, near)):
-                    sums[pl.ds(pl.multiple_of((group + other * 5 + f) * 8, 8), 8), :] = value
-            return inner
-
-        lax.fori_loop(0, 2, one_date, 0)
+                    sums[pl.ds((group + other * 5 + f) * 8, 8), :] = value
+
         wide = jnp.concatenate([sums[pl.ds(chunk, 128, stride=CHUNKS), :] for chunk in range(CHUNKS)], axis=1)
         high = wide.astype(jnp.bfloat16)
         low = (wide - high.astype(jnp.float32)).astype(jnp.bfloat16)
@@ -326,7 +332,8 @@
                 for part in parts_of(direction, distance):
                     if distance:
                         ring(row, direction, distance, part).wait_send()
-                    beside(row, direction, distance, part).wait_send()
+                if distance < 4 or direction == 1:
+                    beside(row, direction, distance).wait_send()
 
     def sent(place, carry):
         to_after(place).wait_send()
@@ -344,9 +351,9 @@
     vmem = pl.BlockSpec(memory_space=pltpu.VMEM)
     dma = pltpu.SemaphoreType.DMA
     tile = (CHUNKS, 128)
-    small = jnp.concatenate([rg_offset, block_order, az_offset])
-    width = -(-small.shape[0] // 128) * 128
-    small = jnp.pad(small, (0, width - small.shape[0]))[None]
+    width = -(-(columns + count + rows) // 128) * 128
+    spare = jnp.zeros((width - columns - count - rows,), jnp.int32)
+    small = jnp.concatenate([rg_offset, block_order, az_offset, spare])[None]
     return pl.pallas_call(
         body,
         out_shape=jax.ShapeDtypeStruct((2, dates, dates * count, rows, columns), jnp.float32),
@@ -355,7 +362,8 @@
         scratch_shapes=[
             pltpu.VMEM((count, 2, dates, lines, *tile), jnp.bfloat16),
             pltpu.VMEM((2, dates, lines, *tile), jnp.float32),
-            pltpu.VMEM((5, total, *tile), jnp.float32),
+            pltpu.VMEM((dates, 5, total, *tile), jnp.float32),
+            pltpu.VMEM((dates, 5, rows + 1, *tile), jnp.float32),
             pltpu.VMEM((128 * CHUNKS, 128), jnp.float32),
             pltpu.VMEM((samples, columns), jnp.bfloat16),
             pltpu.VMEM((dates, rows, columns), jnp.float32),
@@ -363,12 +371,13 @@
             pltpu.VMEM((count, 24, columns), jnp.float32),
             pltpu.VMEM((count, 24, columns), jnp.float32),
             pltpu.SMEM((1, width), jnp.int32),
+            pltpu.SMEM((3 * rows,), jnp.int32),
             pltpu.VMEM((4, 8, 128), jnp.float32),
             pltpu.VMEM((2, 8, 128), jnp.float32),
             pltpu.VMEM((2, 8, 128), jnp.float32),
             dma((2, 2, 4, 2)), dma((2, 2, 4, 2)),
             dma((2,)), dma((2,)),
-            dma((count, 2)), dma((count, 2)),
+            dma((count,)), dma((count,)),
             dma((2,)), dma((2,)),
             dma((2, count)), dma((2, count)),
             dma((2,)),

time: 74.3 us -> 73.4 us (0.988)
  Pallas kernels: 71.1 us -> 70.1 us
    pallas_call x1, Pallas kernels: 71.1 us -> 70.1 us  [on_device(): pl.pallas_call(body, out_shape=jax.ShapeDtypeStruct((2, dates, dates * co...]
where the time goes in v2:
time: 73.4 us; the launch traced here: 73.2 us
  Pallas kernels  70.1 us (96%)
  local copies, waits for them, and re-layouts  2.32 us (3%)
  other arithmetic  0.79 us (1%)
    pallas_call x1, Pallas kernels, on_device(): pl.pallas_call(body, out_shape=jax.ShapeDtypeStruct((2, dates, dates * co...  70.1 us
    unnamed x2, local copies, waits for them, and re-layouts  2.31 us

profile of v2, /device:TPU:1, one launch (start us, length us, event | category | flops | bytes accessed | tf_op | source)
XLA Modules:
  0.0 73.2 jit_solution(2354503361474816589)
XLA Ops:
  0.0 0.8 %pad_add_fusion = s32[384]{0:T(512)S(1)} fusion(s32[88]{0:T(128)S(1)} %broadcast_in_dim.6, s32[8]{0:T(128)} %param.6, s32[32]{0:T(128)} %param.5, s32[256]{0:T(256)} %param.7), kind=kLoop, calls=%fused_computation | loop fusion | flops 1152 | bytes 3072 | tf_op jit(solution)/shard_map/concatenate | solution.py:356
  0.8 1.0 %copy.5 = bf16[16,8,8,128]{3,2,1,0:T(8,128)(2,1)S(1)} copy(bf16[16,8,8,128]{3,1,2,0:T(8,128)(2,1)} %bitcast.6) | data formatting | bytes 524288
  1.8 70.1 %shard_map.46 = f32[2,2,64,8,256]{4,3,2,1,0:T(8,128)S(1)} custom-call(s32[1,384]{1,0:T(1,128)S(1)} %broadcast_in_dim.7.small, bf16[2,2,32,8,128]{4,3,2,1,0:T(8,128)(2,1)S(1)} %bitcast.5), custom_call_target="tpu_custom_call" | custom-call | tf_op jit(solution)/shard_map/pallas_call | solution.py:357
  71.9 1.3 %copy.7 = f32[2,2,64,8,256]{4,3,2,1,0:T(8,128)} copy(f32[2,2,64,8,256]{4,3,2,1,0:T(8,128)S(1)} %shard_map.46) | data formatting | bytes 4194304
  (2 shorter events, 0.0 us)

commit v3 on v2

--- a/solution.py
+++ b/solution.py
@@ -29,26 +29,26 @@
     (1, 0, 4, 0), (1, 0, 4, 1),
 ]
 SLOT = {block: place for place, block in enumerate(BLOCKS)}
-FIRST = -2
+FIRST = -3
 LAG = 10
 EVENTS = {
-    -2: [("ring", 0, 1, 0)],
-    -1: [("ring", 0, 1, 1)],
+    -3: [("ring", 0, 1, 0)],
+    -2: [("ring", 0, 1, 1)],
     0: [("offsets",)],
-    2: [("across", 0)],
-    3: [("ring", 0, 2, 0)],
-    4: [("ring", 0, 2, 1)],
-    6: [("across", 1)],
-    8: [("ring", 1, 1, 0)],
-    10: [("ring", 0, 3, 0)],
-    12: [("ring", 0, 3, 1)],
-    14: [("ring", 1, 1, 1)],
-    16: [("ring", 1, 2, 0)],
-    19: [("ring", 0, 4, 0)],
-    21: [("ring", 1, 2, 1)],
-    24: [("ring", 1, 3, 0)],
-    26: [("ring", 1, 3, 1)],
-    30: [("ring", 1, 4, 0)],
+    1: [("across", 0)],
+    2: [("ring", 0, 2, 0)],
+    3: [("ring", 0, 2, 1)],
+    5: [("across", 1)],
+    7: [("ring", 1, 1, 0)],
+    9: [("ring", 0, 3, 0)],
+    11: [("ring", 0, 3, 1)],
+    13: [("ring", 1, 1, 1)],
+    15: [("ring", 1, 2, 0)],
+    18: [("ring", 0, 4, 0)],
+    20: [("ring", 1, 2, 1)],
+    23: [("ring", 1, 3, 0)],
+    25: [("ring", 1, 3, 1)],
+    29: [("ring", 1, 4, 0)],
 }
 for place, (row, direction, distance, sibling) in enumerate(BLOCKS):
     if sibling:
@@ -173,9 +173,9 @@
             beside(*what).wait_recv()
 
     for part in (0, 1):
-        across(part).start()
         for direction in (0, 1):
             ring(0, direction, 1, part).start()
+        across(part).start()
     local.start()
     beside(0, 0, 0).start()
     to_scalars.wait()

time: 73.4 us -> 72.8 us (level)
  no operation moved by 1% of the time
where the time goes in v3:
time: 72.8 us
  Pallas kernels  69.6 us (96%)
  local copies, waits for them, and re-layouts  2.32 us (3%)
  other arithmetic  0.79 us (1%)
    pallas_call x1, Pallas kernels, on_device(): pl.pallas_call(body, out_shape=jax.ShapeDtypeStruct((2, dates, dates * co...  69.6 us
    unnamed x2, local copies, waits for them, and re-layouts  2.31 us

profile of v3, /device:TPU:1, one launch (start us, length us, event | category | flops | bytes accessed | tf_op | source)
XLA Modules:
  0.0 72.8 jit_solution(16782352488303787653)
XLA Ops:
  0.0 0.8 %pad_add_fusion = s32[384]{0:T(512)S(1)} fusion(s32[88]{0:T(128)S(1)} %broadcast_in_dim.6, s32[8]{0:T(128)} %param.6, s32[32]{0:T(128)} %param.5, s32[256]{0:T(256)} %param.7), kind=kLoop, calls=%fused_computation | loop fusion | flops 1152 | bytes 3072 | tf_op jit(solution)/shard_map/concatenate | solution.py:356
  0.8 1.0 %copy.5 = bf16[16,8,8,128]{3,2,1,0:T(8,128)(2,1)S(1)} copy(bf16[16,8,8,128]{3,1,2,0:T(8,128)(2,1)} %bitcast.6) | data formatting | bytes 524288
  1.8 69.6 %shard_map.46 = f32[2,2,64,8,256]{4,3,2,1,0:T(8,128)S(1)} custom-call(s32[1,384]{1,0:T(1,128)S(1)} %broadcast_in_dim.7.small, bf16[2,2,32,8,128]{4,3,2,1,0:T(8,128)(2,1)S(1)} %bitcast.5), custom_call_target="tpu_custom_call" | custom-call | tf_op jit(solution)/shard_map/pallas_call | solution.py:357
  71.5 1.3 %copy.7 = f32[2,2,64,8,256]{4,3,2,1,0:T(8,128)} copy(f32[2,2,64,8,256]{4,3,2,1,0:T(8,128)S(1)} %shard_map.46) | data formatting | bytes 4194304
  (2 shorter events, 0.0 us)

commit v4 on v3

--- a/solution.py
+++ b/solution.py
@@ -29,26 +29,26 @@
     (1, 0, 4, 0), (1, 0, 4, 1),
 ]
 SLOT = {block: place for place, block in enumerate(BLOCKS)}
-FIRST = -3
+FIRST = -4
 LAG = 10
 EVENTS = {
-    -3: [("ring", 0, 1, 0)],
-    -2: [("ring", 0, 1, 1)],
-    0: [("offsets",)],
-    1: [("across", 0)],
-    2: [("ring", 0, 2, 0)],
-    3: [("ring", 0, 2, 1)],
-    5: [("across", 1)],
-    7: [("ring", 1, 1, 0)],
-    9: [("ring", 0, 3, 0)],
-    11: [("ring", 0, 3, 1)],
-    13: [("ring", 1, 1, 1)],
-    15: [("ring", 1, 2, 0)],
-    18: [("ring", 0, 4, 0)],
-    20: [("ring", 1, 2, 1)],
-    23: [("ring", 1, 3, 0)],
-    25: [("ring", 1, 3, 1)],
-    29: [("ring", 1, 4, 0)],
+    -4: [("ring", 0, 1, 0)],
+    -3: [("ring", 0, 1, 1)],
+    -1: [("offsets",)],
+    0: [("across", 0)],
+    1: [("ring", 0, 2, 0)],
+    2: [("ring", 0, 2, 1)],
+    4: [("across", 1)],
+    6: [("ring", 1, 1, 0)],
+    8: [("ring", 0, 3, 0)],
+    10: [("ring", 0, 3, 1)],
+    12: [("ring", 1, 1, 1)],
+    14: [("ring", 1, 2, 0)],
+    17: [("ring", 0, 4, 0)],
+    19: [("ring", 1, 2, 1)],
+    22: [("ring", 1, 3, 0)],
+    24: [("ring", 1, 3, 1)],
+    28: [("ring", 1, 4, 0)],
 }
 for place, (row, direction, distance, sibling) in enumerate(BLOCKS):
     if sibling:

time: 72.8 us -> 72.6 us (level)
  no operation moved by 1% of the time
where the time goes in v4:
time: 72.6 us; the launch traced here: 72.4 us
  Pallas kernels  69.3 us (95%)
  local copies, waits for them, and re-layouts  2.32 us (3%)
  other arithmetic  0.79 us (1%)
    pallas_call x1, Pallas kernels, on_device(): pl.pallas_call(body, out_shape=jax.ShapeDtypeStruct((2, dates, dates * co...  69.3 us
    unnamed x2, local copies, waits for them, and re-layouts  2.31 us

profile of v4, /device:TPU:1, one launch (start us, length us, event | category | flops | bytes accessed | tf_op | source)
XLA Modules:
  0.0 72.4 jit_solution(15670770570306741863)
XLA Ops:
  0.0 0.8 %pad_add_fusion = s32[384]{0:T(512)S(1)} fusion(s32[88]{0:T(128)S(1)} %broadcast_in_dim.6, s32[8]{0:T(128)} %param.6, s32[32]{0:T(128)} %param.5, s32[256]{0:T(256)} %param.7), kind=kLoop, calls=%fused_computation | loop fusion | flops 1152 | bytes 3072 | tf_op jit(solution)/shard_map/concatenate | solution.py:356
  0.8 1.0 %copy.5 = bf16[16,8,8,128]{3,2,1,0:T(8,128)(2,1)S(1)} copy(bf16[16,8,8,128]{3,1,2,0:T(8,128)(2,1)} %bitcast.6) | data formatting | bytes 524288
  1.8 69.3 %shard_map.46 = f32[2,2,64,8,256]{4,3,2,1,0:T(8,128)S(1)} custom-call(s32[1,384]{1,0:T(1,128)S(1)} %broadcast_in_dim.7.small, bf16[2,2,32,8,128]{4,3,2,1,0:T(8,128)(2,1)S(1)} %bitcast.5), custom_call_target="tpu_custom_call" | custom-call | tf_op jit(solution)/shard_map/pallas_call | solution.py:357
  71.1 1.3 %copy.7 = f32[2,2,64,8,256]{4,3,2,1,0:T(8,128)} copy(f32[2,2,64,8,256]{4,3,2,1,0:T(8,128)S(1)} %shard_map.46) | data formatting | bytes 4194304
  (2 shorter events, 0.0 us)
